TPU v7x, 32 devices: a whole 2x2x4 slice. The times are simulated.
32 devices in a mesh: dp: 8 (over y, x, core), mp: 4 (over z).
Axes of the slice: x: 2, y: 2, z: 4, core: 2. Of those that a mesh axis runs over, the one named last changes fastest.
Arguments:
- tokens: bfloat16 [2048, 3072], P('dp'), may hold values from -16 to 16
- weight: bfloat16 [3072, 3072], P(None, 'mp'), may hold values from -0.109375 to 0.109375
- norm_gain: float32 [128], replicated, may hold values from 0.1 to 1.9
- upstream: bfloat16 [2048, 3072], P('dp', 'mp'), may hold values from -0.176776695 to 0.176776695
Outputs:
- perturbation: float32 [3072, 3072], P('dp', 'mp')
- sharp_grad: float32 [3072, 3072], P('dp', 'mp')
All inputs are finite; a program needn't handle non-finite values.
Results may differ from a plain program's by a relative error of at most 0.0028.
Values may be sent and summed in bfloat16 or wider, within the bound.
A program may use at most 64 MiB of HBM per device.

v0:
```python
import math

import jax
import jax.numpy as jnp
from jax import lax
from jax.sharding import PartitionSpec as P

radius_coef = 0.004


def head_backward(queries, upstream, norm_gain):
    head_dim = norm_gain.shape[0]
    count = queries.shape[0]
    grouped = queries.reshape(count, -1, head_dim)
    centred = grouped - jnp.mean(grouped, axis=-1, keepdims=True)
    inverse = lax.rsqrt(jnp.mean(centred * centred, axis=-1, keepdims=True) + 1e-06)
    normed = centred * inverse
    scaled = upstream.astype(jnp.float32).reshape(count, -1, head_dim) * norm_gain
    result = (
        scaled
        - jnp.mean(scaled, axis=-1, keepdims=True)
        - normed * jnp.mean(scaled * normed, axis=-1, keepdims=True)
    ) * inverse
    return result.reshape(count, -1).astype(jnp.bfloat16)


def left_product(left, right):
    return lax.dot_general(
        left, right, (((0,), (0,)), ((), ())), preferred_element_type=jnp.float32
    )


def per_device(tokens, weight, norm_gain, upstream):
    rows_own = weight.shape[0] // lax.axis_size("dp")
    radius = radius_coef * math.sqrt(weight.shape[0] * weight.shape[1] * lax.axis_size("mp"))
    row_start = lax.axis_index("dp") * rows_own
    first = jnp.dot(tokens, weight, preferred_element_type=jnp.float32)
    first_grad = head_backward(first, upstream, norm_gain)
    rounded = left_product(tokens, first_grad).astype(jnp.bfloat16)
    rounded = lax.optimization_barrier(rounded)
    owned = lax.psum_scatter(rounded.astype(jnp.float32), "dp", scatter_dimension=0, tiled=True)
    local_total = jnp.sum(owned * owned)
    total = lax.psum(local_total, ("dp", "mp"))
    perturbation = owned * (radius / (jnp.sqrt(total) + 1e-12))
    own_weight = lax.dynamic_slice_in_dim(weight, row_start, rows_own, 0)
    own_perturbed = (own_weight.astype(jnp.float32) + perturbation).astype(jnp.bfloat16)
    second = jnp.dot(
        tokens,
        lax.all_gather(own_perturbed, "dp", axis=0, tiled=True),
        preferred_element_type=jnp.float32,
    )
    second_grad = head_backward(second, upstream, norm_gain)
    sharp_grad = lax.psum_scatter(
        left_product(tokens, second_grad), "dp", scatter_dimension=0, tiled=True
    )
    return (perturbation, sharp_grad)


def solution(mesh):
    in_specs = (P("dp", None), P(None, "mp"), P(), P("dp", "mp"))
    out_specs = (P("dp", "mp"), P("dp", "mp"))
    return jax.shard_map(
        per_device, mesh=mesh, in_specs=in_specs, out_specs=out_specs, check_vma=False
    )
```

profile of v0, /device:TPU:1, one launch (start us, length us, event | category | flops | bytes accessed | tf_op | source)
XLA Modules:
  0.0 306.6 jit_solution(11388283779399683206)
XLA Ops:
  7.2 1.4 copy-done
  8.6 3.7 %fusion.3 = f32[256,768]{1,0:T(8,128)S(1)} fusion(bf16[256,3072]{1,0:T(8,128)(2,1)S(1)} %copy-done, bf16[3072,768]{1,0:T(8,128)(2,1)} %param.5), kind=kOutput, calls=%fused_computation.26 | convolution fusion | flops 1207959552 | bytes 7077888 | tf_op jit(solution)/shard_map/dot_general | solution.py:37
  14.9 1.0 multiply_reduce_fusion.5
  16.4 0.9 sub.50
  17.4 1.4 copy.11
  18.8 0.8 mul.120
  19.5 1.1 copy.15
  20.7 0.8 mul.115
  21.5 1.1 copy.14
  22.6 0.9 sub.53
  23.6 2.3 copy.13
  25.9 3.2 %fusion = bf16[3072,768]{0,1:T(8,128)(2,1)S(1)} fusion(bf16[256,3072]{1,0:T(8,128)(2,1)S(1)} %copy-done, f32[256,768]{1,0:T(8,128)} %copy.14, f32[256,768]{1,0:T(8,128)} %copy.15, f32[256,768]{1,0:T(8,128)S(1)} %copy-done.7, f32[256,768]{1,0:T(8,128)} %copy.13, f32[256,768]{1,0:T(8,128)S(1)} %copy.11, f32[768]{0:T(1024)S(1)} %broadcast_bitcast_fusion, ...), kind=kOutput, calls=%fused_computation.2 | convolution fusion | flops 1212088320 | bytes 10619904 | tf_op jit(solution)/shard_map/dot_general | solution.py:28
  29.0 4.9 %convert_element_type.29 = f32[3072,768]{0,1:T(8,128)} convert(bf16[3072,768]{0,1:T(8,128)(2,1)S(1)} %fusion) | non-fusion elementwise | flops 2359296 | bytes 14155776 | tf_op jit(solution)/shard_map/convert_element_type | solution.py:41
  34.0 1.9 constant_dynamic-slice_fusion
  36.0 76.7 %reduce-scatter.3.cloned.1.call-done = f32[384,768]{0,1:T(8,128)} async-done(((f32[3072,768]{0,1:T(8,128)}), f32[384,768]{0,1:T(8,128)}) %reduce-scatter.3.cloned.1.call-update) | async-done | bytes 1179664 | tf_op jit(solution)/shard_map/reduce_scatter | solution.py:41
  112.6 2.4 multiply_reduce_fusion
  115.0 2.1 copy.27
  117.1 39.0 %psum.7 = f32[]{:T(128)} all-reduce(f32[]{:T(128)} %multiply_reduce_fusion), channel_id=1, replica_groups=mesh['dp'=8,'mp'=4] {'dp','mp'}, use_global_device_ids=true, to_apply=%region_6.0 | all-reduce | flops 1 | bytes 8 | tf_op jit(solution)/shard_map/psum | solution.py:43
  156.9 2.4 add_convert_fusion
  159.4 41.8 %all-gather.2.cloned.1.call-done = bf16[3072,768]{0,1:T(8,128)(2,1)} async-done(((bf16[384,768]{0,1:T(8,128)(2,1)}), bf16[3072,768]{0,1:T(8,128)(2,1)}) %all-gather.2.cloned.1.call-update) | async-done | bytes 4718608 | tf_op jit(solution)/shard_map/all_gather | solution.py:49
  201.2 4.6 %convolution_bitcast_fusion.1 = f32[256,768]{1,0:T(8,128)} fusion(bf16[3072,768]{0,1:T(8,128)(2,1)} %all-gather.2.cloned.1.call-done, bf16[256,3072]{1,0:T(8,128)(2,1)S(1)} %copy-done), kind=kOutput, calls=%fused_computation.3 | convolution fusion | flops 1207959552 | bytes 7077888 | tf_op jit(solution)/shard_map/dot_general | solution.py:47
  205.8 1.4 copy.19
  207.4 1.3 multiply_reduce_fusion.1
  208.8 1.2 copy.22
  210.0 1.2 copy.21
  211.2 0.9 sub.58
  212.1 2.3 copy.20
  214.4 6.8 %convolution_bitcast_fusion = f32[3072,768]{0,1:T(8,128)} fusion(bf16[256,3072]{1,0:T(8,128)(2,1)S(1)} %copy-done, f32[256,768]{1,0:T(8,128)} %copy.21, f32[256,768]{1,0:T(8,128)} %copy.22, f32[256,768]{1,0:T(8,128)S(1)} %copy-done.8, f32[256,768]{1,0:T(8,128)} %copy.20, f32[256,768]{1,0:T(8,128)S(1)} %copy.11, f32[768]{0:T(1024)S(1)} %broadcast_bitcast_fusion, ...), kind=kOutput, calls=%fused_computation | convolution fusion | flops 1209729024 | bytes 15338496 | tf_op jit(solution)/shard_map/dot_general | solution.py:28
  221.3 1.2 copy-done.2
  222.5 1.4 copy.24
  223.9 73.5 %reduce-scatter.5.cloned.1.call-done = f32[384,768]{0,1:T(8,128)} async-done(((f32[3072,768]{0,1:T(8,128)}), f32[384,768]{0,1:T(8,128)}) %reduce-scatter.5.cloned.1.call-update) | async-done | bytes 1179664 | tf_op jit(solution)/shard_map/reduce_scatter | solution.py:53
  297.4 2.7 copy.25
  (39 shorter events, 3.6 us)
Async XLA Ops:
  7.2 1.4 copy-start
  7.2 105.5 %reduce-scatter.3.cloned.1.call-start = ((), (), s32[]{:S(2)}) async-start(), calls=%async_computation.2 | async-start | bytes 10616832 | tf_op jit(solution)/shard_map/reduce_scatter | solution.py:41
  12.3 1.8 copy-start.6
  12.3 2.4 copy-start.4
  12.6 2.3 copy-start.9
  14.9 3.9 %copy-start.1 = (f32[256,768]{0,1:T(8,128)}, f32[256,768]{0,1:T(8,128)S(1)}, u32[]{:S(2)}) copy-start(f32[256,768]{0,1:T(8,128)S(1)} %copy.10) | copy-start | bytes 2359300
  22.6 3.3 %copy-start.7 = (f32[256,768]{1,0:T(8,128)S(1)}, f32[256,768]{1,0:T(8,128)}, u32[]{:S(2)}) copy-start(f32[256,768]{1,0:T(8,128)} %copy-done.6) | copy-start | bytes 2359300
  34.0 167.2 %all-gather.2.cloned.1.call-start = ((), (), s32[]{:S(2)}) async-start(), calls=%async_computation.3 | async-start | bytes 5308416 | tf_op jit(solution)/shard_map/all_gather | solution.py:49
  112.6 44.3 %copy-start.3 = (f32[384,768]{0,1:T(8,128)S(1)}, f32[384,768]{0,1:T(8,128)}, u32[]{:S(2)}) copy-start(f32[384,768]{0,1:T(8,128)} %reduce-scatter.3.cloned.1.call-done) | copy-start | bytes 3538948
  159.3 138.1 %reduce-scatter.5.cloned.1.call-start = ((), (), s32[]{:S(2)}) async-start(), calls=%async_computation.4 | async-start | bytes 10616832 | tf_op jit(solution)/shard_map/reduce_scatter | solution.py:53
  211.2 3.2 %copy-start.5 = (bf16[256,768]{1,0:T(8,128)(2,1)S(1)}, bf16[256,768]{1,0:T(8,128)(2,1)}, u32[]{:S(2)}) copy-start(bf16[256,768]{1,0:T(8,128)(2,1)} %param.7) | copy-start | bytes 1179652
  211.2 3.2 %copy-start.8 = (f32[256,768]{1,0:T(8,128)S(1)}, f32[256,768]{1,0:T(8,128)}, u32[]{:S(2)}) copy-start(f32[256,768]{1,0:T(8,128)} %convolution_bitcast_fusion.1) | copy-start | bytes 2359300
  221.2 1.3 copy-start.2
Sparse Core Ops, SparseCore 0:
  34.1 78.4 reduce-scatter.2
  159.5 41.6 all-gather.1
  221.4 75.9 reduce-scatter.4
where the time goes:
time: 308 us; the launch traced here: 307 us
  waiting for transfers between devices  192 us (62%)
  blocking collectives  39 us (13%)
  local copies, waits for them, and re-layouts  27.6 us (9%)
  matrix products  18.3 us (6%)
  other arithmetic  14.8 us (5%)
  between operations  14.7 us (5%)
    reduce_scatter x1, waiting for transfers between devices, per_device(): lax.psum_scatter(rounded.astype(jnp.float32), 'dp', scatter_dimension=0,...  76.7 us
    reduce_scatter x1, waiting for transfers between devices, per_device(): lax.psum_scatter(left_product(tokens, second_grad), 'dp', scatter_dimensi...  73.5 us
    all_gather x1, waiting for transfers between devices, per_device(): lax.all_gather(own_perturbed, 'dp', axis=0, tiled=True)  41.8 us
    psum x1, blocking collectives, per_device(): total = lax.psum(local_total, ('dp', 'mp'))  39 us
    dot_general x2, matrix products, left_product(): lax.dot_general(left, right, (((0,), (0,)), ((), ())), preferred_element_...  9.96 us
    unnamed x23, local copies, waits for them, and re-layouts  8.79 us
    sub x4, local copies, waits for them, and re-layouts, head_backward(): centred = grouped - jnp.mean(grouped, axis=-1, keepdims=True)  6.49 us
  transfers between devices with their start and end apart: 3, of which 3 were waited for; matrix products, arithmetic and copies ran while one was open for 1% of the time, Pallas kernels for 0%

commit v1 on v0

--- a/solution.py
+++ b/solution.py
@@ -1,11 +1,17 @@
+import functools
 import math
 
 import jax
 import jax.numpy as jnp
 from jax import lax
+from jax.experimental import pallas as pl
+from jax.experimental.pallas import tpu as pltpu
 from jax.sharding import PartitionSpec as P
 
 radius_coef = 0.004
+F32 = jnp.float32
+BF16 = jnp.bfloat16
+MESH = pl.DeviceIdType.MESH
 
 
 def head_backward(queries, upstream, norm_gain):
@@ -30,7 +36,7 @@
     )
 
 
-def per_device(tokens, weight, norm_gain, upstream):
+def general_step(tokens, weight, norm_gain, upstream):
     rows_own = weight.shape[0] // lax.axis_size("dp")
     radius = radius_coef * math.sqrt(weight.shape[0] * weight.shape[1] * lax.axis_size("mp"))
     row_start = lax.axis_index("dp") * rows_own
@@ -56,9 +62,270 @@
     return (perturbation, sharp_grad)
 
 
+def cube_kernel(
+    radius, n_mp,
+    tok_ref, w_ref, gain_ref, up_ref,
+    pert_ref, sharp_ref,
+    tok_t, query, grad, keep_x, keep_y,
+    core_out, core_in, x_out, x_in, y_out, y_in,
+    core_out2, core_in2, x_out2, x_in2, y_out2, y_in2,
+    gathered, total_dp, total_mp,
+    send_sem, recv_sem,
+):
+    shards, rows, n_tok = tok_t.shape
+    half = rows // 2
+    head_dim = gain_ref.shape[1]
+    me = lax.axis_index("dp")
+    z = lax.axis_index("mp")
+    y, x, c = me // 4, (me // 2) % 2, me % 2
+    oy, ox, oc = 1 - y, 1 - x, 1 - c
+
+    def at(yy, xx, cc):
+        return (yy * 2 + xx) * 2 + cc
+
+    partner, x_peer, y_peer = at(y, x, oc), at(y, ox, c), at(oy, x, c)
+    diagonal = at(oy, ox, c)
+    dp_peers = [
+        partner, x_peer, y_peer, at(y, ox, oc), at(oy, x, oc), diagonal, at(oy, ox, oc)
+    ]
+    mp_peers = [lax.rem(z + k, n_mp) for k in range(1, n_mp)]
+
+    barrier = pltpu.get_barrier_semaphore()
+    for peer in dp_peers:
+        pl.semaphore_signal(barrier, inc=1, device_id={"dp": peer}, device_id_type=MESH)
+    for peer in mp_peers:
+        pl.semaphore_signal(barrier, inc=1, device_id={"mp": peer}, device_id_type=MESH)
+
+    started = []
+
+    def send(source, target, device):
+        index = len(started)
+        copy = pltpu.make_async_remote_copy(
+            src_ref=source, dst_ref=target,
+            send_sem=send_sem.at[index], recv_sem=recv_sem.at[index],
+            device_id=device, device_id_type=MESH,
+        )
+        copy.start()
+        started.append(copy)
+        return copy
+
+    def rows_of(shard):
+        return pl.ds(pl.multiple_of(shard * rows, rows), rows)
+
+    def backward():
+        for head in range(query.shape[1] // head_dim):
+            columns = pl.ds(head * head_dim, head_dim)
+            values = query[:, columns]
+            centred = values - jnp.mean(values, axis=-1, keepdims=True)
+            inverse = lax.rsqrt(jnp.mean(centred * centred, axis=-1, keepdims=True) + 1e-06)
+            normed = centred * inverse
+            scaled = up_ref[:, columns].astype(F32) * gain_ref[...]
+            result = (
+                scaled
+                - jnp.mean(scaled, axis=-1, keepdims=True)
+                - normed * jnp.mean(scaled * normed, axis=-1, keepdims=True)
+            ) * inverse
+            grad[:, columns] = result.astype(BF16)
+
+    def product(shard):
+        return jnp.dot(tok_t[shard], grad[...], preferred_element_type=F32)
+
+    def reduce_scatter(out_ref, c_out, c_in, xo, xi, yo, yi, rounded):
+        chips = [(oy, ox), (y, ox), (oy, x), (y, x)]
+        low, high = pl.ds(0, half), pl.ds(half, half)
+        core_copies = []
+
+        def to_partner(i):
+            c_out[i] = product(at(*chips[i], oc)).astype(c_out.dtype)
+            core_copies.append(send(c_out.at[i], c_in.at[i], {"dp": partner}))
+
+        def chip_sum(i):
+            mine = product(at(*chips[i], c))
+            if rounded:
+                mine = mine.astype(BF16).astype(F32)
+            core_copies[i].wait_recv()
+            return mine + c_in[i].astype(F32)
+
+        to_partner(0)
+        to_partner(1)
+        value = chip_sum(0)
+        xo[0] = value[:half].astype(BF16)
+        x0 = send(xo.at[0], xi.at[0], {"dp": x_peer})
+        yo[0] = value[half:].astype(BF16)
+        y0 = send(yo.at[0], yi.at[0], {"dp": y_peer})
+        to_partner(2)
+        value = chip_sum(1)
+        xo[1] = value[:half].astype(BF16)
+        x1 = send(xo.at[1], xi.at[1], {"dp": x_peer})
+        keep_x[...] = value[half:]
+        to_partner(3)
+        value = chip_sum(2)
+        yo[1] = value[half:].astype(BF16)
+        y1 = send(yo.at[1], yi.at[1], {"dp": y_peer})
+        keep_y[...] = value[:half]
+        out_ref[...] = chip_sum(3)
+        y0.wait_recv()
+        xo[2] = (keep_x[...] + yi[0].astype(F32)).astype(BF16)
+        x2 = send(xo.at[2], xi.at[2], {"dp": x_peer})
+        x0.wait_recv()
+        yo[2] = (keep_y[...] + xi[0].astype(F32)).astype(BF16)
+        y2 = send(yo.at[2], yi.at[2], {"dp": y_peer})
+        x1.wait_recv()
+        y1.wait_recv()
+        out_ref[low] += xi[1].astype(F32)
+        out_ref[high] += yi[1].astype(F32)
+        x2.wait_recv()
+        y2.wait_recv()
+        out_ref[low] += yi[2].astype(F32)
+        out_ref[high] += xi[2].astype(F32)
+
+    for shard in range(shards):
+        columns = pl.ds(shard * rows, rows)
+        part = jnp.dot(tok_ref[:, columns], w_ref[columns, :], preferred_element_type=F32)
+        if shard == 0:
+            query[...] = part
+        else:
+            query[...] += part
+        tok_t[shard] = tok_ref[:, columns].T
+    backward()
+    pl.semaphore_wait(barrier, len(dp_peers) + len(mp_peers))
+
+    reduce_scatter(pert_ref, core_out, core_in, x_out, x_in, y_out, y_in, True)
+
+    squares = pert_ref[...]
+    squares = squares * squares
+    squares = jnp.sum(squares.reshape(rows // 8, 8, squares.shape[1]), axis=0)
+    folded = squares[:, :128]
+    for tile in range(1, squares.shape[1] // 128):
+        folded = folded + squares[:, tile * 128:(tile + 1) * 128]
+    total_dp[me] = folded
+    dp_copies = [send(total_dp.at[me], total_dp.at[me], {"dp": peer}) for peer in dp_peers]
+
+    gathered[me] = pert_ref[...].astype(BF16)
+
+    def piece(shard, which):
+        return gathered.at[shard, pl.ds(which * half, half)]
+
+    def pass_on(shard, which, device):
+        return send(piece(shard, which), piece(shard, which), {"dp": device})
+
+    ax0 = pass_on(me, 0, x_peer)
+    ay0 = pass_on(me, 1, y_peer)
+    own = send(gathered.at[me], gathered.at[me], {"dp": partner})
+    ax1 = pass_on(me, 1, x_peer)
+    ay1 = pass_on(me, 0, y_peer)
+
+    for copy in dp_copies:
+        copy.wait_recv()
+    folded = total_dp[0]
+    for shard in range(1, shards):
+        folded = folded + total_dp[shard]
+    total_mp[z] = folded
+    mp_copies = [send(total_mp.at[z], total_mp.at[z], {"mp": peer}) for peer in mp_peers]
+
+    ax0.wait_recv()
+    ay2 = pass_on(x_peer, 0, y_peer)
+    fwd = [pass_on(x_peer, 0, partner)]
+    ay0.wait_recv()
+    ax2 = pass_on(y_peer, 1, x_peer)
+    fwd.append(pass_on(y_peer, 1, partner))
+
+    for copy in mp_copies:
+        copy.wait_recv()
+    folded = total_mp[0]
+    for index in range(1, n_mp):
+        folded = folded + total_mp[index]
+    scale = radius / (jnp.sqrt(jnp.sum(folded, keepdims=True)) + 1e-12)
+
+    def second_part(shard, begin=False):
+        index = rows_of(shard)
+        moved = w_ref[index, :].astype(F32) + gathered[shard].astype(F32) * scale
+        part = jnp.dot(tok_ref[:, index], moved.astype(BF16), preferred_element_type=F32)
+        if begin:
+            query[...] = part
+        else:
+            query[...] += part
+
+    second_part(me, True)
+    own.wait_recv()
+    second_part(partner)
+    pert_ref[...] = pert_ref[...] * scale
+    ax1.wait_recv()
+    fwd.append(pass_on(x_peer, 1, partner))
+    ay1.wait_recv()
+    fwd.append(pass_on(y_peer, 0, partner))
+    second_part(x_peer)
+    second_part(y_peer)
+    fwd[0].wait_recv()
+    fwd[2].wait_recv()
+    second_part(at(y, ox, oc))
+    fwd[1].wait_recv()
+    fwd[3].wait_recv()
+    second_part(at(oy, x, oc))
+    ax2.wait_recv()
+    fwd.append(pass_on(diagonal, 1, partner))
+    ay2.wait_recv()
+    fwd.append(pass_on(diagonal, 0, partner))
+    second_part(diagonal)
+    fwd[4].wait_recv()
+    fwd[5].wait_recv()
+    second_part(at(oy, ox, oc))
+
+    backward()
+    reduce_scatter(sharp_ref, core_out2, core_in2, x_out2, x_in2, y_out2, y_in2, False)
+    for copy in started:
+        copy.wait_send()
+
+
+def cube_step(n_dp, n_mp, tokens, weight, norm_gain, upstream):
+    n_tok, feat = tokens.shape
+    columns = weight.shape[1]
+    rows = feat // n_dp
+    half = rows // 2
+    radius = radius_coef * math.sqrt(feat * columns * n_mp)
+    copies = 2 * 10 + 13 + (n_dp - 1) + (n_mp - 1)
+
+    def exchange(core_type):
+        return [
+            pltpu.VMEM((4, rows, columns), core_type),
+            pltpu.VMEM((4, rows, columns), core_type),
+        ] + [pltpu.VMEM((3, half, columns), BF16)] * 4
+
+    vmem = pl.BlockSpec(memory_space=pltpu.VMEM)
+    owned = jax.ShapeDtypeStruct((rows, columns), F32)
+    return pl.pallas_call(
+        functools.partial(cube_kernel, radius, n_mp),
+        out_shape=(owned, owned),
+        in_specs=[vmem] * 4,
+        out_specs=(vmem, vmem),
+        scratch_shapes=[
+            pltpu.VMEM((n_dp, rows, n_tok), BF16),
+            pltpu.VMEM((n_tok, columns), F32),
+            pltpu.VMEM((n_tok, columns), BF16),
+            pltpu.VMEM((half, columns), F32),
+            pltpu.VMEM((half, columns), F32),
+        ]
+        + exchange(BF16)
+        + exchange(F32)
+        + [
+            pltpu.VMEM((n_dp, rows, columns), BF16),
+            pltpu.VMEM((n_dp, 8, 128), F32),
+            pltpu.VMEM((n_mp, 8, 128), F32),
+            pltpu.SemaphoreType.DMA((copies,)),
+            pltpu.SemaphoreType.DMA((copies,)),
+        ],
+        compiler_params=pltpu.CompilerParams(
+            collective_id=0, has_side_effects=True, vmem_limit_bytes=60 * 1024 * 1024
+        ),
+        name="cube_step",
+    )(tokens, weight, norm_gain.reshape(1, -1), upstream)
+
+
 def solution(mesh):
+    n_dp, n_mp = mesh.shape["dp"], mesh.shape["mp"]
+    step = functools.partial(cube_step, n_dp, n_mp) if n_dp == 8 else general_step
     in_specs = (P("dp", None), P(None, "mp"), P(), P("dp", "mp"))
     out_specs = (P("dp", "mp"), P("dp", "mp"))
     return jax.shard_map(
-        per_device, mesh=mesh, in_specs=in_specs, out_specs=out_specs, check_vma=False
+        step, mesh=mesh, in_specs=in_specs, out_specs=out_specs, check_vma=False
     )

time: 308 us -> 86.2 us (0.28)
  waiting for transfers between devices: 192 us -> 0 us
  Pallas kernels: 0 us -> 80.4 us
  blocking collectives: 39 us -> 0 us
  local copies, waits for them, and re-layouts: 27.6 us -> 3.47 us
  matrix products: 18.3 us -> 0 us
  other arithmetic: 14.8 us -> 0 us
  between operations: 14.7 us -> 0.65 us
    reduce_scatter x2 -> x0, waiting for transfers between devices: 150 us -> none  [the longest x1 76.7 us: per_device(): lax.psum_scatter(rounded.astype(jnp.float32), 'dp', scatter_dimension=0,...]
    pallas_call x0 -> x1, Pallas kernels: none -> 80.4 us  [cube_step(): pl.pallas_call(functools.partial(cube_kernel, radius, n_mp), out_shape=(o...]
    all_gather x1 -> x0, waiting for transfers between devices: 41.8 us -> none  [per_device(): lax.all_gather(own_perturbed, 'dp', axis=0, tiled=True)]
    psum x1 -> x0, blocking collectives: 39 us -> none  [per_device(): total = lax.psum(local_total, ('dp', 'mp'))]
    dot_general x4 -> x0, matrix products: 18.3 us -> none  [the longest x2 9.96 us: left_product(): lax.dot_general(left, right, (((0,), (0,)), ((), ())), preferred_element_...]
    sub x6 -> x0, local copies, waits for them, and re-layouts: 8.82 us -> none  [the longest x4 6.49 us: head_backward(): centred = grouped - jnp.mean(grouped, axis=-1, keepdims=True)]
    convert_element_type x2 -> x0, other arithmetic: 7.35 us -> none  [the longest x1 4.93 us: per_device(): rounded.astype(jnp.float32)]
    mul x9 -> x0, local copies, waits for them, and re-layouts: 6.26 us -> none  [the longest x4 3.15 us: head_backward(): normed * jnp.mean(scaled * normed, axis=-1, keepdims=True)]
  transfers between devices with their start and end apart: 3 -> 0, of which waited for: 3 -> 0; matrix products, arithmetic and copies ran while one was open for 1% -> 0% of each run, Pallas kernels for 0% -> 0%
where the time goes in v1:
time: 86.2 us; the launch traced here: 84.5 us
  Pallas kernels  80.4 us (93%)
  local copies, waits for them, and re-layouts  3.47 us (4%)
    pallas_call x1, Pallas kernels, cube_step(): pl.pallas_call(functools.partial(cube_kernel, radius, n_mp), out_shape=(o...  80.4 us
    unnamed x4, local copies, waits for them, and re-layouts  3.47 us

profile of v1, /device:TPU:1, one launch (start us, length us, event | category | flops | bytes accessed | tf_op | source)
XLA Modules:
  0.0 84.5 jit_solution(3821235024086214898)
XLA Ops:
  0.6 80.4 %cube_step.1 = (f32[384,768]{1,0:T(8,128)}, f32[384,768]{1,0:T(8,128)}) custom-call(bf16[256,3072]{1,0:T(8,128)(2,1)} %tok_ref.1, bf16[3072,768]{1,0:T(8,128)(2,1)} %w_ref.1, f32[1,128]{1,0:T(1,128)} %bitcast.1, bf16[256,768]{1,0:T(8,128)(2,1)} %up_ref.1), custom_call_target="tpu_custom_call" | custom-call | tf_op jit(solution)/shard_map/cube_step/pallas_call | solution.py:296
  81.0 0.0 copy-start
  81.0 2.5 %copy.8 = f32[384,768]{1,0:T(8,128)} copy(f32[384,768]{1,0:T(8,128)} %get-tuple-element.4) | data formatting | bytes 2359296
  83.5 0.0 copy-done
  83.5 1.0 %copy.9 = f32[384,768]{1,0:T(8,128)} copy(f32[384,768]{1,0:T(8,128)S(1)} %copy-done) | data formatting | bytes 2359296
Async XLA Ops:
  81.0 2.5 %copy-start = (f32[384,768]{1,0:T(8,128)S(1)}, f32[384,768]{1,0:T(8,128)}, u32[]{:S(2)}) copy-start(f32[384,768]{1,0:T(8,128)} %get-tuple-element.5) | copy-start | bytes 3538948

commit v2 on v1

v2 whole, which is shorter than its diff:
```python
import functools
import math

import jax
import jax.numpy as jnp
from jax import lax
from jax.experimental import pallas as pl
from jax.experimental.pallas import tpu as pltpu
from jax.sharding import PartitionSpec as P

radius_coef = 0.004
F32 = jnp.float32
BF16 = jnp.bfloat16
MESH = pl.DeviceIdType.MESH


def head_backward(queries, upstream, norm_gain):
    head_dim = norm_gain.shape[0]
    count = queries.shape[0]
    grouped = queries.reshape(count, -1, head_dim)
    centred = grouped - jnp.mean(grouped, axis=-1, keepdims=True)
    inverse = lax.rsqrt(jnp.mean(centred * centred, axis=-1, keepdims=True) + 1e-06)
    normed = centred * inverse
    scaled = upstream.astype(jnp.float32).reshape(count, -1, head_dim) * norm_gain
    result = (
        scaled
        - jnp.mean(scaled, axis=-1, keepdims=True)
        - normed * jnp.mean(scaled * normed, axis=-1, keepdims=True)
    ) * inverse
    return result.reshape(count, -1).astype(jnp.bfloat16)


def left_product(left, right):
    return lax.dot_general(
        left, right, (((0,), (0,)), ((), ())), preferred_element_type=jnp.float32
    )


def general_step(tokens, weight, norm_gain, upstream):
    rows_own = weight.shape[0] // lax.axis_size("dp")
    radius = radius_coef * math.sqrt(weight.shape[0] * weight.shape[1] * lax.axis_size("mp"))
    row_start = lax.axis_index("dp") * rows_own
    first = jnp.dot(tokens, weight, preferred_element_type=jnp.float32)
    first_grad = head_backward(first, upstream, norm_gain)
    rounded = left_product(tokens, first_grad).astype(jnp.bfloat16)
    rounded = lax.optimization_barrier(rounded)
    owned = lax.psum_scatter(rounded.astype(jnp.float32), "dp", scatter_dimension=0, tiled=True)
    local_total = jnp.sum(owned * owned)
    total = lax.psum(local_total, ("dp", "mp"))
    perturbation = owned * (radius / (jnp.sqrt(total) + 1e-12))
    own_weight = lax.dynamic_slice_in_dim(weight, row_start, rows_own, 0)
    own_perturbed = (own_weight.astype(jnp.float32) + perturbation).astype(jnp.bfloat16)
    second = jnp.dot(
        tokens,
        lax.all_gather(own_perturbed, "dp", axis=0, tiled=True),
        preferred_element_type=jnp.float32,
    )
    second_grad = head_backward(second, upstream, norm_gain)
    sharp_grad = lax.psum_scatter(
        left_product(tokens, second_grad), "dp", scatter_dimension=0, tiled=True
    )
    return (perturbation, sharp_grad)


def cube_kernel(
    radius, n_mp,
    tok_ref, w_hbm, gain_ref, up_ref,
    pert_ref, sharp_ref,
    weight, query, moved, delta, keep_x, keep_y,
    tok_own, tok_t, grads, grads2,
    core_out, core_in, x_out, x_in, y_out, y_in,
    total_dp, total_mp,
    load_sem, send_sem, recv_sem,
):
    shards, n_tok, rows = tok_own.shape
    half = n_tok // 2
    head_dim = gain_ref.shape[1]
    me = lax.axis_index("dp")
    z = lax.axis_index("mp")
    y, x, c = me // 4, (me // 2) % 2, me % 2
    oy, ox, oc = 1 - y, 1 - x, 1 - c

    loads = []
    for shard in range(shards):
        part = pl.ds(shard * rows, rows)
        loads.append(
            pltpu.make_async_copy(w_hbm.at[part], weight.at[part], load_sem.at[shard])
        )
        loads[-1].start()

    def at(yy, xx, cc):
        return (yy * 2 + xx) * 2 + cc

    partner, x_peer, y_peer = at(y, x, oc), at(y, ox, c), at(oy, x, c)
    x_cross, y_cross = at(y, ox, oc), at(oy, x, oc)
    diagonal, far = at(oy, ox, c), at(oy, ox, oc)
    remote = [x_peer, y_peer, x_cross, y_cross, diagonal, far]
    dp_peers = [partner] + remote
    mp_peers = [lax.rem(z + k, n_mp) for k in range(1, n_mp)]
    parity = z % 2
    z_pair = z + 1 - 2 * parity

    barrier = pltpu.get_barrier_semaphore()
    for peer in dp_peers:
        pl.semaphore_signal(barrier, inc=1, device_id={"dp": peer}, device_id_type=MESH)
    for peer in mp_peers:
        pl.semaphore_signal(barrier, inc=1, device_id={"mp": peer}, device_id_type=MESH)

    started = []

    def send(source, target, device):
        index = len(started)
        copy = pltpu.make_async_remote_copy(
            src_ref=source, dst_ref=target,
            send_sem=send_sem.at[index], recv_sem=recv_sem.at[index],
            device_id=device, device_id_type=MESH,
        )
        copy.start()
        started.append(copy)
        return copy

    def columns_of(shard):
        return pl.ds(pl.multiple_of(shard * rows, rows), rows)

    def backward(out, low):
        span = pl.ds(low, half)
        for head in range(query.shape[1] // head_dim):
            columns = pl.ds(head * head_dim, head_dim)
            values = query[span, columns]
            centred = values - jnp.mean(values, axis=-1, keepdims=True)
            inverse = lax.rsqrt(jnp.mean(centred * centred, axis=-1, keepdims=True) + 1e-06)
            normed = centred * inverse
            scaled = up_ref[span, columns].astype(F32) * gain_ref[...]
            result = (
                scaled
                - jnp.mean(scaled, axis=-1, keepdims=True)
                - normed * jnp.mean(scaled * normed, axis=-1, keepdims=True)
            ) * inverse
            out[me, span, columns] = result.astype(BF16)

    def gather(buffer, ready, consume):
        def pass_on(shard, which, device):
            block = buffer.at[shard, pl.ds(which * half, half)]
            return send(block, block, {"dp": device})

        backward(buffer, 0)
        x0 = pass_on(me, 0, x_peer)
        backward(buffer, half)
        y0 = pass_on(me, 1, y_peer)
        x1 = pass_on(me, 1, x_peer)
        y1 = pass_on(me, 0, y_peer)
        own = send(buffer.at[me], buffer.at[me], {"dp": partner})
        ready()
        consume(me)
        x0.wait_recv()
        y2 = pass_on(x_peer, 0, y_peer)
        y0.wait_recv()
        x2 = pass_on(y_peer, 1, x_peer)
        f0 = pass_on(x_peer, 0, partner)
        f1 = pass_on(y_peer, 1, partner)
        own.wait_recv()
        consume(partner)
        x1.wait_recv()
        f2 = pass_on(x_peer, 1, partner)
        y1.wait_recv()
        f3 = pass_on(y_peer, 0, partner)
        consume(x_peer)
        consume(y_peer)
        f0.wait_recv()
        f2.wait_recv()
        consume(x_cross)
        f1.wait_recv()
        f3.wait_recv()
        consume(y_cross)
        x2.wait_recv()
        f4 = pass_on(diagonal, 1, partner)
        y2.wait_recv()
        f5 = pass_on(diagonal, 0, partner)
        consume(diagonal)
        f4.wait_recv()
        f5.wait_recv()
        consume(far)

    def product(shard):
        return jnp.dot(tok_own[shard], moved[...], preferred_element_type=F32)

    def reduce_scatter(between):
        chips = [(oy, ox), (y, ox), (oy, x), (y, x)]
        low, high = pl.ds(0, half), pl.ds(half, half)
        core_copies = []

        def to_partner(i):
            core_out[i] = product(at(*chips[i], oc)).astype(BF16)
            core_copies.append(send(core_out.at[i], core_in.at[i], {"dp": partner}))

        def chip_sum(i):
            mine = product(at(*chips[i], c))
            core_copies[i].wait_recv()
            return mine + core_in[i].astype(F32)

        to_partner(0)
        to_partner(1)
        value = chip_sum(0)
        x_out[0] = value[:half].astype(BF16)
        x0 = send(x_out.at[0], x_in.at[0], {"dp": x_peer})
        y_out[0] = value[half:].astype(BF16)
        y0 = send(y_out.at[0], y_in.at[0], {"dp": y_peer})
        to_partner(2)
        value = chip_sum(1)
        x_out[1] = value[:half].astype(BF16)
        x1 = send(x_out.at[1], x_in.at[1], {"dp": x_peer})
        keep_x[...] = value[half:]
        to_partner(3)
        value = chip_sum(2)
        y_out[1] = value[half:].astype(BF16)
        y1 = send(y_out.at[1], y_in.at[1], {"dp": y_peer})
        keep_y[...] = value[:half]
        between()
        y0.wait_recv()
        x_out[2] = (keep_x[...] + y_in[0].astype(F32)).astype(BF16)
        x2 = send(x_out.at[2], x_in.at[2], {"dp": x_peer})
        x0.wait_recv()
        y_out[2] = (keep_y[...] + x_in[0].astype(F32)).astype(BF16)
        y2 = send(y_out.at[2], y_in.at[2], {"dp": y_peer})
        delta[...] = chip_sum(3)
        x1.wait_recv()
        y1.wait_recv()
        delta[low] += x_in[1].astype(F32)
        delta[high] += y_in[1].astype(F32)
        y2.wait_recv()
        delta[low] += y_in[2].astype(F32)
        x2.wait_recv()
        delta[high] += x_in[2].astype(F32)

    pl.semaphore_wait(barrier, len(dp_peers) + len(mp_peers))
    share = pl.ds(pl.multiple_of(parity * half, half), half)
    brought = [
        send(tok_ref.at[share, columns_of(peer)], tok_own.at[me, share], {"dp": peer})
        for peer in remote
    ]
    from_partner = send(
        tok_ref.at[:, columns_of(partner)], tok_own.at[me], {"dp": partner}
    )
    passed = []

    def pass_pair(index):
        brought[index].wait_recv()
        block = tok_own.at[remote[index], share]
        passed.append(send(block, block, {"mp": z_pair}))

    for shard in range(shards):
        columns = pl.ds(shard * rows, rows)
        loads[shard].wait()
        part = jnp.dot(tok_ref[:, columns], weight[columns, :], preferred_element_type=F32)
        if shard == 0:
            query[...] = part
        else:
            query[...] += part
    tok_own[me] = tok_ref[:, columns_of(me)]
    for index in range(4):
        pass_pair(index)

    def add_ascent(shard):
        if shard is not me:
            if shard is partner:
                from_partner.wait_recv()
            else:
                for index, peer in enumerate(remote):
                    if peer is shard:
                        passed[index].wait_recv()
        turned = tok_own[shard].T
        tok_t[shard] = turned
        part = jnp.dot(turned, grads[shard], preferred_element_type=F32)
        part = part.astype(BF16).astype(F32)
        if shard is me:
            pert_ref[...] = part
        else:
            pert_ref[...] += part

    def pass_rest():
        for index in range(4, 6):
            pass_pair(index)

    gather(grads, pass_rest, add_ascent)

    squares = pert_ref[...]
    moved[...] = squares.astype(BF16)
    squares = squares * squares
    squares = jnp.sum(squares.reshape(rows // 8, 8, squares.shape[1]), axis=0)
    folded = squares[:, :128]
    for tile in range(1, squares.shape[1] // 128):
        folded = folded + squares[:, tile * 128:(tile + 1) * 128]
    total_dp[me] = folded
    dp_copies = [send(total_dp.at[me], total_dp.at[me], {"dp": peer}) for peer in dp_peers]
    mp_copies = []

    def over_planes():
        for copy in dp_copies:
            copy.wait_recv()
        summed = total_dp[0]
        for shard in range(1, shards):
            summed = summed + total_dp[shard]
        total_mp[z] = summed
        for peer in mp_peers:
            mp_copies.append(send(total_mp.at[z], total_mp.at[z], {"mp": peer}))

    reduce_scatter(over_planes)
    for copy in mp_copies:
        copy.wait_recv()
    summed = total_mp[0]
    for index in range(1, n_mp):
        summed = summed + total_mp[index]
    scale = radius / (jnp.sqrt(jnp.sum(summed, keepdims=True)) + 1e-12)

    query[...] += delta[...] * scale

    def write_perturbation():
        pert_ref[...] = pert_ref[...] * scale

    def add_sharp(shard):
        part = jnp.dot(tok_t[shard], grads2[shard], preferred_element_type=F32)
        if shard is me:
            sharp_ref[...] = part
        else:
            sharp_ref[...] += part

    gather(grads2, write_perturbation, add_sharp)
    for copy in started:
        copy.wait_send()


def cube_step(n_dp, n_mp, tokens, weight, norm_gain, upstream):
    n_tok, feat = tokens.shape
    columns = weight.shape[1]
    rows = feat // n_dp
    half = n_tok // 2
    radius = radius_coef * math.sqrt(feat * columns * n_mp)
    copies = 13 + 2 * 13 + 10 + (n_dp - 1) + (n_mp - 1)
    vmem = pl.BlockSpec(memory_space=pltpu.VMEM)
    owned = jax.ShapeDtypeStruct((rows, columns), F32)
    return pl.pallas_call(
        functools.partial(cube_kernel, radius, n_mp),
        out_shape=(owned, owned),
        in_specs=[vmem, pl.BlockSpec(memory_space=pl.ANY), vmem, vmem],
        out_specs=(vmem, vmem),
        scratch_shapes=[
            pltpu.VMEM((feat, columns), BF16),
            pltpu.VMEM((n_tok, columns), F32),
            pltpu.VMEM((rows, columns), BF16),
            pltpu.VMEM((n_tok, columns), F32),
            pltpu.VMEM((half, columns), F32),
            pltpu.VMEM((half, columns), F32),
            pltpu.VMEM((n_dp, n_tok, rows), BF16),
            pltpu.VMEM((n_dp, rows, n_tok), BF16),
            pltpu.VMEM((n_dp, n_tok, columns), BF16),
            pltpu.VMEM((n_dp, n_tok, columns), BF16),
            pltpu.VMEM((4, n_tok, columns), BF16),
            pltpu.VMEM((4, n_tok, columns), BF16),
        ]
        + [pltpu.VMEM((3, half, columns), BF16)] * 4
        + [
            pltpu.VMEM((n_dp, 8, 128), F32),
            pltpu.VMEM((n_mp, 8, 128), F32),
            pltpu.SemaphoreType.DMA((n_dp,)),
            pltpu.SemaphoreType.DMA((copies,)),
            pltpu.SemaphoreType.DMA((copies,)),
        ],
        compiler_params=pltpu.CompilerParams(
            collective_id=0, has_side_effects=True, vmem_limit_bytes=60 * 1024 * 1024
        ),
        name="cube_step",
    )(tokens, weight, norm_gain.reshape(1, -1), upstream)


def solution(mesh):
    n_dp, n_mp = mesh.shape["dp"], mesh.shape["mp"]
    step = functools.partial(cube_step, n_dp, n_mp) if n_dp == 8 and n_mp % 2 == 0 else general_step
    in_specs = (P("dp", None), P(None, "mp"), P(), P("dp", "mp"))
    out_specs = (P("dp", "mp"), P("dp", "mp"))
    return jax.shard_map(
        step, mesh=mesh, in_specs=in_specs, out_specs=out_specs, check_vma=False
    )
```

time: 86.2 us -> 72.5 us (0.84); the launches traced: 84.5 us -> 72.3 us
  Pallas kernels: 80.4 us -> 68.2 us
    pallas_call x1, Pallas kernels: 80.4 us -> 68.2 us  [cube_step(): pl.pallas_call(functools.partial(cube_kernel, radius, n_mp), out_shape=(o...]
where the time goes in v2:
time: 72.5 us; the launch traced here: 72.3 us
  Pallas kernels  68.2 us (94%)
  local copies, waits for them, and re-layouts  3.47 us (5%)
    pallas_call x1, Pallas kernels, cube_step(): pl.pallas_call(functools.partial(cube_kernel, radius, n_mp), out_shape=(o...  68.2 us
    unnamed x4, local copies, waits for them, and re-layouts  3.47 us

profile of v2, /device:TPU:1, one launch (start us, length us, event | category | flops | bytes accessed | tf_op | source)
XLA Modules:
  0.0 72.3 jit_solution(177119977970716593)
XLA Ops:
  0.6 68.2 %cube_step.1 = (f32[384,768]{1,0:T(8,128)}, f32[384,768]{1,0:T(8,128)}) custom-call(bf16[256,3072]{1,0:T(8,128)(2,1)} %tok_ref.1, bf16[3072,768]{1,0:T(8,128)(2,1)} %w_hbm.1, f32[1,128]{1,0:T(1,128)} %bitcast.1, bf16[256,768]{1,0:T(8,128)(2,1)} %up_ref.1), custom_call_target="tpu_custom_call" | custom-call | tf_op jit(solution)/shard_map/cube_step/pallas_call | solution.py:341
  68.8 0.0 copy-start
  68.8 2.5 %copy.8 = f32[384,768]{1,0:T(8,128)} copy(f32[384,768]{1,0:T(8,128)} %get-tuple-element.4) | data formatting | bytes 2359296
  71.3 0.0 copy-done
  71.3 1.0 %copy.9 = f32[384,768]{1,0:T(8,128)} copy(f32[384,768]{1,0:T(8,128)S(1)} %copy-done) | data formatting | bytes 2359296
Async XLA Ops:
  68.8 2.5 %copy-start = (f32[384,768]{1,0:T(8,128)S(1)}, f32[384,768]{1,0:T(8,128)}, u32[]{:S(2)}) copy-start(f32[384,768]{1,0:T(8,128)} %get-tuple-element.5) | copy-start | bytes 3538948

commit v3 on v2

--- a/solution.py
+++ b/solution.py
@@ -74,6 +74,7 @@
 ):
     shards, n_tok, rows = tok_own.shape
     half = n_tok // 2
+    width = query.shape[1] // 2
     head_dim = gain_ref.shape[1]
     me = lax.axis_index("dp")
     z = lax.axis_index("mp")
@@ -122,10 +123,10 @@
     def columns_of(shard):
         return pl.ds(pl.multiple_of(shard * rows, rows), rows)
 
-    def backward(out, low):
+    def backward(out, part, low):
         span = pl.ds(low, half)
-        for head in range(query.shape[1] // head_dim):
-            columns = pl.ds(head * head_dim, head_dim)
+        for head in range(width // head_dim):
+            columns = pl.ds(part * width + head * head_dim, head_dim)
             values = query[span, columns]
             centred = values - jnp.mean(values, axis=-1, keepdims=True)
             inverse = lax.rsqrt(jnp.mean(centred * centred, axis=-1, keepdims=True) + 1e-06)
@@ -136,101 +137,127 @@
                 - jnp.mean(scaled, axis=-1, keepdims=True)
                 - normed * jnp.mean(scaled * normed, axis=-1, keepdims=True)
             ) * inverse
-            out[me, span, columns] = result.astype(BF16)
-
-    def gather(buffer, ready, consume):
+            out[part, me, span, pl.ds(head * head_dim, head_dim)] = result.astype(BF16)
+
+    def gather(buffer, part, consume):
         def pass_on(shard, which, device):
-            block = buffer.at[shard, pl.ds(which * half, half)]
+            block = buffer.at[part, shard, pl.ds(which * half, half)]
             return send(block, block, {"dp": device})
 
-        backward(buffer, 0)
+        backward(buffer, part, 0)
         x0 = pass_on(me, 0, x_peer)
-        backward(buffer, half)
+        backward(buffer, part, half)
         y0 = pass_on(me, 1, y_peer)
+        own = send(buffer.at[part, me], buffer.at[part, me], {"dp": partner})
+        yield
         x1 = pass_on(me, 1, x_peer)
         y1 = pass_on(me, 0, y_peer)
-        own = send(buffer.at[me], buffer.at[me], {"dp": partner})
-        ready()
-        consume(me)
+        yield
+        consume(part, me)
+        yield
         x0.wait_recv()
         y2 = pass_on(x_peer, 0, y_peer)
         y0.wait_recv()
         x2 = pass_on(y_peer, 1, x_peer)
         f0 = pass_on(x_peer, 0, partner)
         f1 = pass_on(y_peer, 1, partner)
+        yield
         own.wait_recv()
-        consume(partner)
+        consume(part, partner)
+        yield
         x1.wait_recv()
         f2 = pass_on(x_peer, 1, partner)
         y1.wait_recv()
         f3 = pass_on(y_peer, 0, partner)
-        consume(x_peer)
-        consume(y_peer)
+        consume(part, x_peer)
+        consume(part, y_peer)
+        yield
         f0.wait_recv()
         f2.wait_recv()
-        consume(x_cross)
+        consume(part, x_cross)
         f1.wait_recv()
         f3.wait_recv()
-        consume(y_cross)
+        consume(part, y_cross)
+        yield
         x2.wait_recv()
         f4 = pass_on(diagonal, 1, partner)
         y2.wait_recv()
         f5 = pass_on(diagonal, 0, partner)
-        consume(diagonal)
+        consume(part, diagonal)
+        yield
         f4.wait_recv()
         f5.wait_recv()
-        consume(far)
-
-    def product(shard):
-        return jnp.dot(tok_own[shard], moved[...], preferred_element_type=F32)
-
-    def reduce_scatter(between):
+        consume(part, far)
+        yield
+
+    def product(part, shard):
+        return jnp.dot(tok_own[shard], moved[part], preferred_element_type=F32)
+
+    def reduce_scatter(part):
         chips = [(oy, ox), (y, ox), (oy, x), (y, x)]
         low, high = pl.ds(0, half), pl.ds(half, half)
         core_copies = []
 
         def to_partner(i):
-            core_out[i] = product(at(*chips[i], oc)).astype(BF16)
-            core_copies.append(send(core_out.at[i], core_in.at[i], {"dp": partner}))
+            core_out[part, i] = product(part, at(*chips[i], oc)).astype(BF16)
+            core_copies.append(
+                send(core_out.at[part, i], core_in.at[part, i], {"dp": partner})
+            )
 
         def chip_sum(i):
-            mine = product(at(*chips[i], c))
+            mine = product(part, at(*chips[i], c))
             core_copies[i].wait_recv()
-            return mine + core_in[i].astype(F32)
+            return mine + core_in[part, i].astype(F32)
+
+        def by_x(i):
+            return send(x_out.at[part, i], x_in.at[part, i], {"dp": x_peer})
+
+        def by_y(i):
+            return send(y_out.at[part, i], y_in.at[part, i], {"dp": y_peer})
 
         to_partner(0)
         to_partner(1)
+        yield
         value = chip_sum(0)
-        x_out[0] = value[:half].astype(BF16)
-        x0 = send(x_out.at[0], x_in.at[0], {"dp": x_peer})
-        y_out[0] = value[half:].astype(BF16)
-        y0 = send(y_out.at[0], y_in.at[0], {"dp": y_peer})
+        x_out[part, 0] = value[:half].astype(BF16)
+        x0 = by_x(0)
+        y_out[part, 0] = value[half:].astype(BF16)
+        y0 = by_y(0)
         to_partner(2)
+        yield
         value = chip_sum(1)
-        x_out[1] = value[:half].astype(BF16)
-        x1 = send(x_out.at[1], x_in.at[1], {"dp": x_peer})
-        keep_x[...] = value[half:]
+        x_out[part, 1] = value[:half].astype(BF16)
+        x1 = by_x(1)
+        keep_x[part] = value[half:]
         to_partner(3)
+        yield
         value = chip_sum(2)
-        y_out[1] = value[half:].astype(BF16)
-        y1 = send(y_out.at[1], y_in.at[1], {"dp": y_peer})
-        keep_y[...] = value[:half]
-        between()
+        y_out[part, 1] = value[half:].astype(BF16)
+        y1 = by_y(1)
+        keep_y[part] = value[:half]
+        yield
         y0.wait_recv()
-        x_out[2] = (keep_x[...] + y_in[0].astype(F32)).astype(BF16)
-        x2 = send(x_out.at[2], x_in.at[2], {"dp": x_peer})
+        x_out[part, 2] = (keep_x[part] + y_in[part, 0].astype(F32)).astype(BF16)
+        x2 = by_x(2)
         x0.wait_recv()
-        y_out[2] = (keep_y[...] + x_in[0].astype(F32)).astype(BF16)
-        y2 = send(y_out.at[2], y_in.at[2], {"dp": y_peer})
-        delta[...] = chip_sum(3)
+        y_out[part, 2] = (keep_y[part] + x_in[part, 0].astype(F32)).astype(BF16)
+        y2 = by_y(2)
+        delta[part] = chip_sum(3)
+        yield
         x1.wait_recv()
         y1.wait_recv()
-        delta[low] += x_in[1].astype(F32)
-        delta[high] += y_in[1].astype(F32)
+        delta[part, low] += x_in[part, 1].astype(F32)
+        delta[part, high] += y_in[part, 1].astype(F32)
+        yield
         y2.wait_recv()
-        delta[low] += y_in[2].astype(F32)
+        delta[part, low] += y_in[part, 2].astype(F32)
         x2.wait_recv()
-        delta[high] += x_in[2].astype(F32)
+        delta[part, high] += x_in[part, 2].astype(F32)
+        yield
+
+    def run(phase, steps=1):
+        for _ in range(steps):
+            next(phase)
 
     pl.semaphore_wait(barrier, len(dp_peers) + len(mp_peers))
     share = pl.ds(pl.multiple_of(parity * half, half), half)
@@ -260,31 +287,57 @@
     for index in range(4):
         pass_pair(index)
 
-    def add_ascent(shard):
-        if shard is not me:
+    def columns_in(part):
+        return pl.ds(part * width, width)
+
+    def add_ascent(part, shard):
+        if part == 0:
             if shard is partner:
                 from_partner.wait_recv()
-            else:
-                for index, peer in enumerate(remote):
-                    if peer is shard:
-                        passed[index].wait_recv()
-        turned = tok_own[shard].T
-        tok_t[shard] = turned
-        part = jnp.dot(turned, grads[shard], preferred_element_type=F32)
-        part = part.astype(BF16).astype(F32)
+            for index, peer in enumerate(remote):
+                if peer is shard:
+                    passed[index].wait_recv()
+            turned = tok_own[shard].T
+            tok_t[shard] = turned
+        else:
+            turned = tok_t[shard]
+        value = jnp.dot(turned, grads[part, shard], preferred_element_type=F32)
+        value = value.astype(BF16).astype(F32)
         if shard is me:
-            pert_ref[...] = part
+            pert_ref[:, columns_in(part)] = value
         else:
-            pert_ref[...] += part
-
-    def pass_rest():
-        for index in range(4, 6):
-            pass_pair(index)
-
-    gather(grads, pass_rest, add_ascent)
+            pert_ref[:, columns_in(part)] += value
+
+    def add_sharp(part, shard):
+        value = jnp.dot(tok_t[shard], grads2[part, shard], preferred_element_type=F32)
+        if shard is me:
+            sharp_ref[:, columns_in(part)] = value
+        else:
+            sharp_ref[:, columns_in(part)] += value
+
+    def moved_of(part):
+        moved[part] = pert_ref[:, columns_in(part)].astype(BF16)
+
+    g_a, g_b = gather(grads, 0, add_ascent), gather(grads, 1, add_ascent)
+    run(g_a, 2)
+    run(g_b)
+    for index in range(4, 6):
+        pass_pair(index)
+    run(g_a, 2)
+    run(g_b)
+    run(g_a)
+    run(g_b, 2)
+    run(g_a, 2)
+    run(g_b)
+    run(g_a, 2)
+    moved_of(0)
+    r_a, r_b = reduce_scatter(0), reduce_scatter(1)
+    run(r_a)
+    run(g_b, 2)
+    run(r_a, 2)
+    run(g_b, 2)
 
     squares = pert_ref[...]
-    moved[...] = squares.astype(BF16)
     squares = squares * squares
     squares = jnp.sum(squares.reshape(rows // 8, 8, squares.shape[1]), axis=0)
     folded = squares[:, :128]
@@ -292,19 +345,21 @@
         folded = folded + squares[:, tile * 128:(tile + 1) * 128]
     total_dp[me] = folded
     dp_copies = [send(total_dp.at[me], total_dp.at[me], {"dp": peer}) for peer in dp_peers]
-    mp_copies = []
-
-    def over_planes():
-        for copy in dp_copies:
-            copy.wait_recv()
-        summed = total_dp[0]
-        for shard in range(1, shards):
-            summed = summed + total_dp[shard]
-        total_mp[z] = summed
-        for peer in mp_peers:
-            mp_copies.append(send(total_mp.at[z], total_mp.at[z], {"mp": peer}))
-
-    reduce_scatter(over_planes)
+    moved_of(1)
+    run(r_b)
+    run(r_a, 2)
+    run(r_b, 2)
+    for copy in dp_copies:
+        copy.wait_recv()
+    summed = total_dp[0]
+    for shard in range(1, shards):
+        summed = summed + total_dp[shard]
+    total_mp[z] = summed
+    mp_copies = [send(total_mp.at[z], total_mp.at[z], {"mp": peer}) for peer in mp_peers]
+    run(r_a)
+    run(r_b)
+    run(r_a)
+    run(r_b)
     for copy in mp_copies:
         copy.wait_recv()
     summed = total_mp[0]
@@ -312,19 +367,21 @@
         summed = summed + total_mp[index]
     scale = radius / (jnp.sqrt(jnp.sum(summed, keepdims=True)) + 1e-12)
 
-    query[...] += delta[...] * scale
-
-    def write_perturbation():
-        pert_ref[...] = pert_ref[...] * scale
-
-    def add_sharp(shard):
-        part = jnp.dot(tok_t[shard], grads2[shard], preferred_element_type=F32)
-        if shard is me:
-            sharp_ref[...] = part
-        else:
-            sharp_ref[...] += part
-
-    gather(grads2, write_perturbation, add_sharp)
+    g_a, g_b = gather(grads2, 0, add_sharp), gather(grads2, 1, add_sharp)
+    query[:, columns_in(0)] += delta[0] * scale
+    run(g_a, 2)
+    run(r_b, 2)
+    query[:, columns_in(1)] += delta[1] * scale
+    run(g_b)
+    run(g_a, 2)
+    run(g_b)
+    run(g_a)
+    pert_ref[...] = pert_ref[...] * scale
+    run(g_b, 2)
+    run(g_a, 2)
+    run(g_b)
+    run(g_a, 2)
+    run(g_b, 4)
     for copy in started:
         copy.wait_send()
 
@@ -335,7 +392,8 @@
     rows = feat // n_dp
     half = n_tok // 2
     radius = radius_coef * math.sqrt(feat * columns * n_mp)
-    copies = 13 + 2 * 13 + 10 + (n_dp - 1) + (n_mp - 1)
+    width = columns // 2
+    copies = 13 + 4 * 13 + 2 * 10 + (n_dp - 1) + (n_mp - 1)
     vmem = pl.BlockSpec(memory_space=pltpu.VMEM)
     owned = jax.ShapeDtypeStruct((rows, columns), F32)
     return pl.pallas_call(
@@ -346,18 +404,18 @@
         scratch_shapes=[
             pltpu.VMEM((feat, columns), BF16),
             pltpu.VMEM((n_tok, columns), F32),
-            pltpu.VMEM((rows, columns), BF16),
-            pltpu.VMEM((n_tok, columns), F32),
-            pltpu.VMEM((half, columns), F32),
-            pltpu.VMEM((half, columns), F32),
+            pltpu.VMEM((2, rows, width), BF16),
+            pltpu.VMEM((2, n_tok, width), F32),
+            pltpu.VMEM((2, half, width), F32),
+            pltpu.VMEM((2, half, width), F32),
             pltpu.VMEM((n_dp, n_tok, rows), BF16),
             pltpu.VMEM((n_dp, rows, n_tok), BF16),
-            pltpu.VMEM((n_dp, n_tok, columns), BF16),
-            pltpu.VMEM((n_dp, n_tok, columns), BF16),
-            pltpu.VMEM((4, n_tok, columns), BF16),
-            pltpu.VMEM((4, n_tok, columns), BF16),
+            pltpu.VMEM((2, n_dp, n_tok, width), BF16),
+            pltpu.VMEM((2, n_dp, n_tok, width), BF16),
+            pltpu.VMEM((2, 4, n_tok, width), BF16),
+            pltpu.VMEM((2, 4, n_tok, width), BF16),
         ]
-        + [pltpu.VMEM((3, half, columns), BF16)] * 4
+        + [pltpu.VMEM((2, 3, half, width), BF16)] * 4
         + [
             pltpu.VMEM((n_dp, 8, 128), F32),
             pltpu.VMEM((n_mp, 8, 128), F32),

time: 72.5 us -> 68.9 us (0.950)
  Pallas kernels: 68.2 us -> 64.6 us
    pallas_call x1, Pallas kernels: 68.2 us -> 64.6 us  [cube_step(): pl.pallas_call(functools.partial(cube_kernel, radius, n_mp), out_shape=(o...]
where the time goes in v3:
time: 68.9 us; the launch traced here: 68.7 us
  Pallas kernels  64.6 us (94%)
  local copies, waits for them, and re-layouts  3.47 us (5%)
    pallas_call x1, Pallas kernels, cube_step(): pl.pallas_call(functools.partial(cube_kernel, radius, n_mp), out_shape=(o...  64.6 us
    unnamed x4, local copies, waits for them, and re-layouts  3.47 us

profile of v3, /device:TPU:1, one launch (start us, length us, event | category | flops | bytes accessed | tf_op | source)
XLA Modules:
  0.0 68.7 jit_solution(16353430530408079878)
XLA Ops:
  0.6 64.6 %cube_step.1 = (f32[384,768]{1,0:T(8,128)}, f32[384,768]{1,0:T(8,128)}) custom-call(bf16[256,3072]{1,0:T(8,128)(2,1)} %tok_ref.1, bf16[3072,768]{1,0:T(8,128)(2,1)} %w_hbm.1, f32[1,128]{1,0:T(1,128)} %bitcast.1, bf16[256,768]{1,0:T(8,128)(2,1)} %up_ref.1), custom_call_target="tpu_custom_call" | custom-call | tf_op jit(solution)/shard_map/cube_step/pallas_call | solution.py:399
  65.2 0.0 copy-start
  65.2 2.5 %copy.8 = f32[384,768]{1,0:T(8,128)} copy(f32[384,768]{1,0:T(8,128)} %get-tuple-element.4) | data formatting | bytes 2359296
  67.7 0.0 copy-done
  67.7 1.0 %copy.9 = f32[384,768]{1,0:T(8,128)} copy(f32[384,768]{1,0:T(8,128)S(1)} %copy-done) | data formatting | bytes 2359296
Async XLA Ops:
  65.2 2.5 %copy-start = (f32[384,768]{1,0:T(8,128)S(1)}, f32[384,768]{1,0:T(8,128)}, u32[]{:S(2)}) copy-start(f32[384,768]{1,0:T(8,128)} %get-tuple-element.5) | copy-start | bytes 3538948

commit v4 on v3

--- a/solution.py
+++ b/solution.py
@@ -395,7 +395,7 @@
     width = columns // 2
     copies = 13 + 4 * 13 + 2 * 10 + (n_dp - 1) + (n_mp - 1)
     vmem = pl.BlockSpec(memory_space=pltpu.VMEM)
-    owned = jax.ShapeDtypeStruct((rows, columns), F32)
+    owned = pltpu.VMEM((rows, columns), F32)
     return pl.pallas_call(
         functools.partial(cube_kernel, radius, n_mp),
         out_shape=(owned, owned),

time: 68.9 us -> 66 us (0.958)
  local copies, waits for them, and re-layouts: 3.47 us -> 2.03 us
  Pallas kernels: 64.6 us -> 63.2 us
    unnamed x4 -> x2, local copies, waits for them, and re-layouts: 3.47 us -> 2.03 us
    pallas_call x1, Pallas kernels: 64.6 us -> 63.2 us  [cube_step(): pl.pallas_call(functools.partial(cube_kernel, radius, n_mp), out_shape=(o...]
where the time goes in v4:
time: 66 us; the launch traced here: 65.9 us
  Pallas kernels  63.2 us (96%)
  local copies, waits for them, and re-layouts  2.03 us (3%)
    pallas_call x1, Pallas kernels, cube_step(): pl.pallas_call(functools.partial(cube_kernel, radius, n_mp), out_shape=(o...  63.2 us
    unnamed x2, local copies, waits for them, and re-layouts  2.03 us

profile of v4, /device:TPU:1, one launch (start us, length us, event | category | flops | bytes accessed | tf_op | source)
XLA Modules:
  0.0 65.9 jit_solution(6873910649826651853)
XLA Ops:
  0.6 63.2 %cube_step.1 = (f32[384,768]{1,0:T(8,128)S(1)}, f32[384,768]{1,0:T(8,128)S(1)}) custom-call(bf16[256,3072]{1,0:T(8,128)(2,1)} %tok_ref.1, bf16[3072,768]{1,0:T(8,128)(2,1)} %w_hbm.1, f32[1,128]{1,0:T(1,128)} %bitcast.1, bf16[256,768]{1,0:T(8,128)(2,1)} %up_ref.1), custom_call_target="tpu_custom_call" | custom-call | tf_op jit(solution)/shard_map/cube_step/pallas_call | solution.py:399
  63.8 1.0 %copy.8 = f32[384,768]{1,0:T(8,128)} copy(f32[384,768]{1,0:T(8,128)S(1)} %get-tuple-element.2) | data formatting | bytes 2359296
  64.8 1.0 %copy.9 = f32[384,768]{1,0:T(8,128)} copy(f32[384,768]{1,0:T(8,128)S(1)} %get-tuple-element.3) | data formatting | bytes 2359296
